TPU v7x, 128 devices: a whole 4x4x4 slice. The times are simulated.
128 devices in a mesh: dp: 4 (over x_lo, core), ctx: 32 (over x_hi, y, z).
Axes of the slice: x: 4 (x_hi: 2, x_lo: 2; x = x_hi * 2 + x_lo), y: 4, z: 4, core: 2. Of those that a mesh axis runs over, the one named last changes fastest.
Arguments:
- frames: bfloat16 [4, 160, 16, 16, 512], P('dp', 'ctx'), may hold values from -6 to 6
- stream: bfloat16 [4, 160, 64, 3072], P('dp', 'ctx'), may hold values from -6 to 6
- video_frames: int32 [4], P('dp'), may hold values from 1 to 160
- conv_weight: bfloat16 [3, 3, 3, 512, 512], replicated, may hold values from -0.0546875 to 0.0546875
- latent_weight: bfloat16 [512, 16], replicated, may hold values from -0.25 to 0.25
- embed_weight: bfloat16 [64, 3072], replicated, may hold values from -0.75 to 0.75
- norm_gain: float32 [3072], replicated, may hold values from 0.25 to 1.75
- qkv_weight: bfloat16 [3072, 4608], P('ctx', 'dp'), may hold values from -0.109375 to 0.109375
Outputs:
- section: bfloat16 [4, 160, 16, 16, 512], P('dp', 'ctx')
- mixed: bfloat16 [4, 160, 64, 1536], P('dp', 'ctx')
All inputs are finite; a program needn't handle non-finite values.
Results may differ from a plain program's by a relative error of at most 0.0061.
Values may be sent and summed in bfloat16 or wider, within the bound.
A program may use at most 128 MiB of HBM per device.

v0:
```python
import jax
import jax.numpy as jnp
from jax import lax
from jax.sharding import Mesh
from jax.sharding import PartitionSpec as P

HD = 128
CTX = ("ctx_0", "ctx_1", "ctx_2")


def passed_along(value, axis, steps):
    count = lax.axis_size(axis)
    leading, last = (max(0, -steps), min(count, count - steps))
    return lax.ppermute(value, axis, [(source, source + steps) for source in range(leading, last)])


def from_everyone(array, axis):
    length = lax.axis_size(axis)
    return lax.all_to_all(
        jnp.broadcast_to(array[None], (length, *array.shape)), axis, 0, 0, tiled=True
    )


def laid_out(tiles, dim):
    dims = list(tiles.shape[1:])
    dims[dim] *= tiles.shape[0]
    return jnp.moveaxis(tiles, 0, dim).reshape(dims)


def gathered_copies(array, axis, dim):
    tiles = from_everyone(array, axis)
    return laid_out(tiles, dim)


def all_blocks(array, axes, turns):
    tiles = array[None]
    for k in turns:
        tiles = lax.all_gather(tiles, axes[k], axis=0, tiled=True)
    current = [lax.axis_size(axes[k]) for k in reversed(turns)]
    tiles = tiles.reshape(*current, *array.shape)
    turned = sorted(range(len(turns)), key=lambda place: turns[len(turns) - 1 - place])
    return tiles.transpose(*turned, *range(len(turns), tiles.ndim)).reshape(-1, *array.shape)


def gather_axes(array, axes, turns, dim):
    return laid_out(all_blocks(array, axes, turns), dim)


def attend(lengths, block):
    head_size = block.shape[-1] // 3
    slots = block.shape[1]
    query = block[..., 0:head_size]
    keys = block[..., head_size : 2 * head_size]
    values = block[..., 2 * head_size : 3 * head_size]
    scores = jnp.einsum(
        "gtphd,gsphd->gphts", query, keys, preferred_element_type=jnp.float32
    ) * head_size ** (-0.5)
    frame_ids = jnp.arange(slots, dtype=jnp.int32)
    video = frame_ids[None, :] < lengths[:, None]
    allowed = (
        video[:, :, None] & video[:, None, :] | (frame_ids[:, None] == frame_ids[None, :])[None]
    )
    scores = jnp.where(allowed[:, None, None], scores, -1e30)
    top = jnp.max(scores, axis=-1, keepdims=True)
    expo = jnp.exp(scores - top)
    probs = (expo / jnp.sum(expo, axis=-1, keepdims=True)).astype(jnp.bfloat16)
    out = jnp.einsum(
        "gphts,gsphd->gtphd", probs, values, preferred_element_type=jnp.float32
    ).astype(jnp.bfloat16)
    return lax.all_to_all(out, CTX, split_axis=1, concat_axis=2, tiled=True)


def on_device(
    frames, stream, video_frames, conv_weight, latent_weight, embed_weight, norm_gain, qkv_weight
):
    f_dev, height, width, channels = (
        frames.shape[1],
        frames.shape[2],
        frames.shape[3],
        frames.shape[4],
    )
    width_model = stream.shape[3]
    tokens_frame = stream.shape[2]
    act = jax.nn.silu(frames.astype(jnp.float32)).astype(jnp.bfloat16)
    past = passed_along(act[:, f_dev - 2 :], CTX, 1)
    joined = jnp.concatenate([past, act], axis=1)[0]
    padded = jnp.pad(joined, ((0, 0), (1, 1), (1, 1), (0, 0)))
    length = video_frames[0]
    frame_ids = lax.axis_index(CTX) * f_dev + jnp.arange(f_dev, dtype=jnp.int32)
    cells = f_dev * height * width
    total = jnp.zeros((cells, channels), jnp.float32)
    for lag in range(3):
        part = jnp.zeros((cells, channels), jnp.float32)
        for row in range(3):
            for col in range(3):
                slab = padded[
                    2 - lag : 2 - lag + f_dev, row : row + height, col : col + width, :
                ].reshape(-1, channels)
                part = part + jnp.dot(
                    slab, conv_weight[lag, row, col], preferred_element_type=jnp.float32
                )
        if lag == 0:
            total = part
        else:
            valid = ((frame_ids < length) & (frame_ids >= lag)).astype(jnp.float32)
            total = total + part * jnp.repeat(valid, height * width)[:, None]
    section = (frames.astype(jnp.float32) + total.reshape(frames.shape)).astype(jnp.bfloat16)
    latent = jnp.dot(
        section.reshape(-1, channels), latent_weight, preferred_element_type=jnp.float32
    ).astype(jnp.bfloat16)
    lat_size = latent.shape[1]
    latent = latent.reshape(f_dev, height // 2, 2, width // 2, 2, lat_size).transpose(
        0, 1, 3, 2, 4, 5
    )
    patches = latent.reshape(-1, 4 * lat_size)
    embedded = jnp.dot(patches, embed_weight, preferred_element_type=jnp.float32) + stream.reshape(
        -1, width_model
    ).astype(jnp.float32)
    scale = lax.rsqrt(jnp.mean(embedded * embedded, axis=-1, keepdims=True) + 1e-06)
    normed = (embedded * scale * norm_gain).astype(jnp.bfloat16)
    head_size = HD
    gathered, lengths = (
        gathered_copies(normed.reshape(1, -1, width_model), "dp", 0),
        gathered_copies(video_frames, "dp", 0),
    )
    group_count = gathered.shape[0]
    all_rows = gathered.reshape(-1, width_model)
    qkv = jnp.dot(
        all_rows, gather_axes(qkv_weight, CTX, (0, 1, 2), 0), preferred_element_type=jnp.float32
    )
    qkv = qkv.astype(jnp.bfloat16).reshape(
        group_count, f_dev, tokens_frame, qkv_weight.shape[1] // (3 * head_size), 3 * head_size
    )
    mixed = attend(lengths, lax.all_to_all(qkv, CTX, split_axis=2, concat_axis=1, tiled=True))
    mixed = lax.all_to_all(mixed, "dp", split_axis=0, concat_axis=3, tiled=True)
    return (section, mixed.reshape(1, f_dev, tokens_frame, -1))


def solution(mesh):
    finer = Mesh(mesh.devices.reshape(mesh.shape["dp"], 2, 4, 4), ("dp", "ctx_0", "ctx_1", "ctx_2"))
    return jax.shard_map(
        on_device,
        mesh=finer,
        in_specs=(
            P("dp", CTX, None, None, None),
            P("dp", CTX, None, None),
            P("dp"),
            P(),
            P(),
            P(),
            P(),
            P(CTX, "dp"),
        ),
        out_specs=(P("dp", CTX, None, None, None), P("dp", CTX, None, None)),
        check_vma=False,
    )
```

profile of v0, /device:TPU:1, one launch (start us, length us, event | category | flops | bytes accessed | tf_op | source)
XLA Modules:
  0.0 339.0 jit_solution(1459822168728964891)
XLA Ops:
  7.2 2.2 fusion.9
  9.5 4.4 %collective-permute-start = (bf16[1,2,16,16,512]{4,3,2,1,0:T(8,128)(2,1)S(1)}, bf16[1,2,16,16,512]{4,3,2,1,0:T(8,128)(2,1)S(1)}, u32[]{:S(2)}, u32[]{:S(2)}) collective-permute-start(bf16[1,2,16,16,512]{4,3,2,1,0:T(8,128)(2,1)S(1)} %slice.235), channel_id=1, source_target_pairs={{0,1},{1,2},{2,3},{3,4},{4,5},{5,6},{6,7},{7,8},{8,9},{9,10},{10,1... | collective-permute-start | bytes 1572872 | tf_op jit(solution)/shard_map/ppermute | solution.py:14
  13.9 8.3 %all-gather = bf16[192,1152]{1,0:T(8,128)(2,1)} all-gather(bf16[96,1152]{1,0:T(8,128)(2,1)S(1)} %copy-done.28), channel_id=2, replica_groups=mesh['dp'=4,'ctx_0'=2,'ctx_1'=4,'ctx_2'=4] {'ctx_0'}, dimensions={0}, use_global_device_ids=true | all-gather | bytes 663552 | tf_op jit(solution)/shard_map/all_gather | solution.py:38
  23.1 1.3 collective-permute-done
  24.6 11.2 %pad_slice_fusion = (bf16[5,16,16,512]{3,2,1,0:T(8,128)(2,1)}, bf16[5,16,16,512]{3,2,1,0:T(8,128)(2,1)}, bf16[5,16,16,512]{3,2,1,0:T(8,128)(2,1)}, bf16[5,16,16,...) fusion(bf16[7,16,16,512]{3,2,1,0:T(8,128)(2,1)S(1)} %fusion.15), kind=kLoop, calls=%fused_computation.1 | loop fusion | bytes 26738688 | tf_op jit(solution)/shard_map/slice | solution.py:96
  35.8 3.8 %pad_slice_fusion.1 = (bf16[5,16,16,512]{3,2,1,0:T(8,128)(2,1)}, bf16[5,16,16,512]{3,2,1,0:T(8,128)(2,1)}, bf16[5,16,16,512]{3,2,1,0:T(8,128)(2,1)}, bf16[5,16,1...) fusion(bf16[7,16,16,512]{3,2,1,0:T(8,128)(2,1)S(1)} %fusion.15), kind=kLoop, calls=%fused_computation.2 | loop fusion | bytes 8388608 | tf_op jit(solution)/shard_map/slice | solution.py:96
  41.9 0.9 convolution_add_fusion.24
  43.3 0.9 convolution_add_fusion.23
  44.7 0.9 convolution_add_fusion.22
  45.6 0.9 convolution_add_fusion.21
  46.9 0.9 convolution_add_fusion.20
  48.2 0.9 convolution_add_fusion.19
  49.5 0.9 convolution_add_fusion.18
  50.9 2.4 convolution_add_fusion.17
  54.5 0.8 convolution_add_fusion.15
  58.0 1.3 fusion.19
  59.3 0.9 convolution_add_fusion.13
  60.6 0.9 convolution_add_fusion.12
  62.0 0.9 convolution_add_fusion.11
  63.3 2.4 convolution_add_fusion.10
  67.9 2.4 convolution_add_fusion.6
  70.3 2.5 convolution_add_fusion.5
  72.9 2.0 convolution_add_fusion.4
  74.9 2.0 convolution_add_fusion.3
  76.9 2.1 convolution_add_fusion.2
  79.9 2.0 fusion.4
  81.9 2.0 fusion.2
  84.5 1.0 copy-done.22
  88.1 4.2 %broadcast_in_dim.20 = bf16[4,1,320,3072]{3,2,1,0:T(8,128)(2,1)} broadcast(bf16[320,3072]{1,0:T(8,128)(2,1)S(1)} %multiply_convert_fusion), dimensions={2,3} | broadcast | bytes 9830400 | tf_op jit(solution)/shard_map/broadcast_in_dim | solution.py:20
  92.3 6.9 %all-to-all-start = ((bf16[4,1,320,3072]{3,2,1,0:T(8,128)(2,1)}), bf16[4,1,320,3072]{3,2,1,0:T(8,128)(2,1)}, u32[]{:S(2)}, u32[]{:S(2)}) async-start(bf16[4,1,320,3072]{3,2,1,0:T(8,128)(2,1)} %broadcast_in_dim.20), calls=%async_computation | async-start | bytes 15728640 | tf_op jit(solution)/shard_map/all_to_all | solution.py:19
  99.2 50.1 %all-gather.6.cloned.1.call-done = bf16[32,96,1152]{2,1,0:T(8,128)(2,1)} async-done(((bf16[8,96,1152]{2,1,0:T(8,128)(2,1)}), bf16[32,96,1152]{2,1,0:T(8,128)(2,1)}) %all-gather.6.cloned.1.call-update) | async-done | bytes 7077904 | tf_op jit(solution)/shard_map/all_gather | solution.py:38
  149.3 6.7 %copy.61 = bf16[2,4,4,96,1152]{4,3,2,1,0:T(8,128)(2,1)} copy(bf16[2,4,4,96,1152]{4,3,0,1,2:T(8,128)(2,1)} %bitcast.178) | data formatting | bytes 14155776 | tf_op jit(solution)/shard_map/transpose | solution.py:42
  156.1 29.8 %all-to-all-done = bf16[4,1,320,3072]{3,2,1,0:T(8,128)(2,1)} async-done(((bf16[4,1,320,3072]{3,2,1,0:T(8,128)(2,1)}), bf16[4,1,320,3072]{3,2,1,0:T(8,128)(2,1)}, u32[]{:S(2)}, u32[]{:S(2)}) %all-to-all-start) | async-done | bytes 7864352 | tf_op jit(solution)/shard_map/all_to_all | solution.py:19
  186.4 4.3 %all-to-all-start.2 = ((s32[4,1,1]{2,1,0:T(1,128)}), s32[4,1,1]{2,1,0:T(1,128)S(1)}, u32[]{:S(2)}, u32[]{:S(2)}) async-start(s32[4,1,1]{2,1,0:T(1,128)} %broadcast_in_dim.22), calls=%async_computation.2 | async-start | bytes 4096 | tf_op jit(solution)/shard_map/all_to_all | solution.py:19
  190.8 14.7 %convolution_convert_fusion = bf16[1280,1152]{1,0:T(8,128)(2,1)S(1)} fusion(bf16[1280,3072]{1,0:T(8,128)(2,1)} %bitcast.61, bf16[3072,1152]{1,0:T(8,128)(2,1)} %bitcast.179), kind=kOutput, calls=%fused_computation.25 | convolution fusion | flops 9061171200 | bytes 17891328 | tf_op jit(solution)/shard_map/dot_general | solution.py:128
  205.5 4.3 %reshape.226 = bf16[4,5,64,3,384]{4,3,2,1,0:T(4,128)(2,1)} reshape(bf16[1280,1152]{1,0:T(8,128)(2,1)S(1)} %convolution_convert_fusion) | data formatting | bytes 5898240 | tf_op jit(solution)/shard_map/reshape | solution.py:131
  209.8 7.5 %copy.62 = bf16[4,5,64,3,384]{4,0,3,1,2:T(4,128)(2,1)} copy(bf16[4,5,64,3,384]{4,3,2,1,0:T(4,128)(2,1)} %reshape.226) | data formatting | bytes 5898240 | tf_op jit(solution)/shard_map/reshape | solution.py:131
  217.4 17.6 %all-to-all-start.1 = ((bf16[4,5,64,3,384]{4,0,3,1,2:T(4,128)(2,1)}), bf16[4,5,64,3,384]{4,0,3,1,2:T(4,128)(2,1)S(1)}, u32[]{:S(2)}, u32[]{:S(2)}) async-start(bf16[4,5,64,3,384]{4,0,3,1,2:T(4,128)(2,1)} %copy.62), calls=%async_computation.1 | async-start | bytes 5898240 | tf_op jit(solution)/shard_map/all_to_all | solution.py:134
  235.4 37.3 %all-to-all-done.1 = bf16[4,5,64,3,384]{4,0,3,1,2:T(4,128)(2,1)S(1)} async-done(((bf16[4,5,64,3,384]{4,0,3,1,2:T(4,128)(2,1)}), bf16[4,5,64,3,384]{4,0,3,1,2:T(4,128)(2,1)S(1)}, u32[]{:S(2)}, u32[]{:S(2)}) %all-to-all-start.1) | async-done | bytes 2949152 | tf_op jit(solution)/shard_map/all_to_all | solution.py:134
  272.7 2.3 copy.63
  275.0 2.1 fusion.83
  277.8 1.4 fusion.84
  279.2 1.0 fusion.17
  281.0 25.4 %all_to_all.62 = bf16[4,160,2,3,128]{4,0,3,2,1:T(4,128)(2,1)S(1)} all-to-all(bf16[4,160,2,3,128]{4,0,3,2,1:T(4,128)(2,1)S(1)} %copy.68), channel_id=1, replica_groups=mesh['dp'=4,'ctx_0'=2,'ctx_1'=4,'ctx_2'=4] {'ctx_0','ctx_1','ctx_2'}, dimensions={1} | all-to-all | bytes 1966080 | tf_op jit(solution)/shard_map/all_to_all | solution.py:70
  307.2 1.1 copy.70
  308.3 21.2 %all_to_all.63 = bf16[4,5,64,3,128]{4,2,3,1,0:T(8,128)(2,1)S(1)} all-to-all(bf16[4,5,64,3,128]{4,2,3,1,0:T(8,128)(2,1)S(1)} %bitcast.208), channel_id=1, replica_groups=mesh['dp'=4,'ctx_0'=2,'ctx_1'=4,'ctx_2'=4] {'dp'}, dimensions={0} | all-to-all | bytes 1966080 | tf_op jit(solution)/shard_map/all_to_all | solution.py:135
  329.5 0.8 copy.71
  330.3 1.6 reshape.227
  (106 shorter events, 20.3 us)
Async XLA Ops:
  7.2 79.6 %copy-start = (bf16[64,3072]{1,0:T(8,128)(2,1)S(1)}, bf16[64,3072]{1,0:T(8,128)(2,1)}, u32[]{:S(2)}) copy-start(bf16[64,3072]{1,0:T(8,128)(2,1)} %param.13) | copy-start | bytes 1179652
  7.2 6.7 %copy-start.28 = (bf16[96,1152]{1,0:T(8,128)(2,1)S(1)}, bf16[96,1152]{1,0:T(8,128)(2,1)}, u32[]{:S(2)}) copy-start(bf16[96,1152]{1,0:T(8,128)(2,1)} %param.15) | copy-start | bytes 663556
  7.2 60.6 %all-gather.4.cloned.1.call-start = ((), (), s32[]{:S(2)}) async-start(), calls=%async_computation.5 | async-start | bytes 2211840 | tf_op jit(solution)/shard_map/all_gather | solution.py:38
  9.5 15.0 %collective-permute-start = (bf16[1,2,16,16,512]{4,3,2,1,0:T(8,128)(2,1)S(1)}, bf16[1,2,16,16,512]{4,3,2,1,0:T(8,128)(2,1)S(1)}, u32[]{:S(2)}, u32[]{:S(2)}) collective-permute-start(bf16[1,2,16,16,512]{4,3,2,1,0:T(8,128)(2,1)S(1)} %slice.235), channel_id=1, source_target_pairs={{0,1},{1,2},{2,3},{3,4},{4,5},{5,6},{6,7},{7,8},{8,9},{9,10},{10,1... | collective-permute-start | bytes 1572872 | tf_op jit(solution)/shard_map/ppermute | solution.py:14
  22.2 127.1 %all-gather.6.cloned.1.call-start = ((), (), s32[]{:S(2)}) async-start(), calls=%async_computation.6 | async-start | bytes 8847360 | tf_op jit(solution)/shard_map/all_gather | solution.py:38
  24.4 15.2 %slice-start = ((s8[14155776]{0:T(1024)(128)(4,1)}), s8[4194304]{0:T(1024)(128)(4,1)S(1)}, s32[]{:S(2)}) async-start(s8[14155776]{0:T(1024)(128)(4,1)} %bitcast.173), calls=%async_computation.7 | async-start | bytes 8388608
  24.6 15.1 %slice-start.1 = ((s8[14155776]{0:T(1024)(128)(4,1)}), s8[4194304]{0:T(1024)(128)(4,1)S(1)}, s32[]{:S(2)}) async-start(s8[14155776]{0:T(1024)(128)(4,1)} %bitcast.173), calls=%async_computation.8 | async-start | bytes 8388608
  24.6 15.0 %slice-start.2 = ((s8[14155776]{0:T(1024)(128)(4,1)}), s8[4194304]{0:T(1024)(128)(4,1)S(1)}, s32[]{:S(2)}) async-start(s8[14155776]{0:T(1024)(128)(4,1)} %bitcast.173), calls=%async_computation.9 | async-start | bytes 8388608
  24.6 15.0 %slice-start.3 = ((s8[14155776]{0:T(1024)(128)(4,1)}), s8[1572864]{0:T(1024)(128)(4,1)S(1)}, s32[]{:S(2)}) async-start(s8[14155776]{0:T(1024)(128)(4,1)} %bitcast.173), calls=%async_computation.10 | async-start | bytes 3145728
  40.5 1.4 copy-start.17
  41.9 1.4 copy-start.16
  43.3 1.4 copy-start.15
  45.6 1.3 copy-start.14
  46.9 1.3 copy-start.13
  48.2 1.3 copy-start.12
  49.5 1.3 copy-start.11
  50.9 2.4 copy-start.10
  53.2 1.3 copy-start.9
  54.5 1.3 copy-start.8
  55.8 1.3 copy-start.18
  59.3 1.3 copy-start.7
  60.6 1.3 copy-start.6
  62.0 1.3 copy-start.5
  65.6 1.3 copy-start.4
  67.9 2.4 copy-start.23
  70.3 2.5 copy-start.26
  72.9 2.0 copy-start.25
  74.9 2.0 copy-start.24
  76.9 2.1 copy-start.2
  76.9 2.7 copy-start.3
  76.9 3.0 copy-start.20
  79.9 2.0 copy-start.19
  81.9 2.0 copy-start.21
  84.0 1.6 copy-start.29
  84.5 1.1 copy-start.22
  84.5 2.2 copy-start.27
  86.7 0.8 copy-start.30
  92.3 93.5 %all-to-all-start = ((bf16[4,1,320,3072]{3,2,1,0:T(8,128)(2,1)}), bf16[4,1,320,3072]{3,2,1,0:T(8,128)(2,1)}, u32[]{:S(2)}, u32[]{:S(2)}) async-start(bf16[4,1,320,3072]{3,2,1,0:T(8,128)(2,1)} %broadcast_in_dim.20), calls=%async_computation | async-start | bytes 15728640 | tf_op jit(solution)/shard_map/all_to_all | solution.py:19
  186.4 30.9 %all-to-all-start.2 = ((s32[4,1,1]{2,1,0:T(1,128)}), s32[4,1,1]{2,1,0:T(1,128)S(1)}, u32[]{:S(2)}, u32[]{:S(2)}) async-start(s32[4,1,1]{2,1,0:T(1,128)} %broadcast_in_dim.22), calls=%async_computation.2 | async-start | bytes 4096 | tf_op jit(solution)/shard_map/all_to_all | solution.py:19
  217.4 55.4 %all-to-all-start.1 = ((bf16[4,5,64,3,384]{4,0,3,1,2:T(4,128)(2,1)}), bf16[4,5,64,3,384]{4,0,3,1,2:T(4,128)(2,1)S(1)}, u32[]{:S(2)}, u32[]{:S(2)}) async-start(bf16[4,5,64,3,384]{4,0,3,1,2:T(4,128)(2,1)} %copy.62), calls=%async_computation.1 | async-start | bytes 5898240 | tf_op jit(solution)/shard_map/all_to_all | solution.py:134
  308.3 23.7 %copy-start.1 = (bf16[64,3072]{1,0:T(8,128)(2,1)S(1)}, bf16[64,3072]{1,0:T(8,128)(2,1)}, u32[]{:S(2)}) copy-start(bf16[64,3072]{1,0:T(8,128)(2,1)} %param.13) | copy-start | bytes 1179652
Sparse Core Ops, SparseCore 0:
  22.3 38.4 all-gather.3
  68.0 81.3 all-gather.5
where the time goes:
time: 344 us; the launch traced here: 339 us
  waiting for transfers between devices  119 us (35%)
  local copies, waits for them, and re-layouts  57.4 us (17%)
  blocking collectives  54.9 us (16%)
  matrix products  52.6 us (15%)
  starting transfers between devices  33.3 us (10%)
  between operations  15.6 us (5%)
  other arithmetic  6.67 us (2%)
    all_gather x2, waiting for transfers between devices, all_blocks(): tiles = lax.all_gather(tiles, axes[k], axis=0, tiled=True)  50.1 us
    all_to_all x1, waiting for transfers between devices, on_device(): lax.all_to_all(qkv, CTX, split_axis=2, concat_axis=1, tiled=True)  37.3 us
    dot_general x27, matrix products, on_device(): jnp.dot(slab, conv_weight[lag, row, col], preferred_element_type=jnp.floa...  35 us
    all_to_all x2, waiting for transfers between devices, from_everyone(): lax.all_to_all(jnp.broadcast_to(array[None], (length, *array.shape)), axi...  29.8 us
    all_to_all x1, blocking collectives, attend(): return lax.all_to_all(out, CTX, split_axis=1, concat_axis=2, tiled=True)  25.4 us
    all_to_all x1, blocking collectives, on_device(): mixed = lax.all_to_all(mixed, 'dp', split_axis=0, concat_axis=3, tiled=True)  21.2 us
    all_to_all x1, starting transfers between devices, on_device(): lax.all_to_all(qkv, CTX, split_axis=2, concat_axis=1, tiled=True)  17.6 us
    slice x2, local copies, waits for them, and re-layouts, on_device(): padded[2 - lag:2 - lag + f_dev, row:row + height, col:col + width, :]  15 us
  transfers between devices with their start and end apart: 6, of which 4 were waited for; matrix products, arithmetic and copies ran while one was open for 27% of the time, Pallas kernels for 0%

commit v1 on v0

--- a/solution.py
+++ b/solution.py
@@ -35,7 +35,9 @@
 def all_blocks(array, axes, turns):
     tiles = array[None]
     for k in turns:
-        tiles = lax.all_gather(tiles, axes[k], axis=0, tiled=True)
+        tiles = jnp.concatenate(
+            lax.all_to_all(jnp.stack([tiles] * lax.axis_size(axes[k])), axes[k], 0, 0), axis=0
+        )
     current = [lax.axis_size(axes[k]) for k in reversed(turns)]
     tiles = tiles.reshape(*current, *array.shape)
     turned = sorted(range(len(turns)), key=lambda place: turns[len(turns) - 1 - place])

time: 344 us -> 400 us (1.16)
  waiting for transfers between devices: 119 us -> 180 us
  between operations: 15.6 us -> 2.21 us
  starting transfers between devices: 33.3 us -> 43 us
  blocking collectives: 54.9 us -> 46.6 us
  local copies, waits for them, and re-layouts: 57.4 us -> 62.1 us
    all_to_all x0 -> x3, waiting for transfers between devices: none -> 62.7 us  [all_blocks(): lax.all_to_all(jnp.stack([tiles] * lax.axis_size(axes[k])), axes[k], 0, 0)]
    all_gather x2 -> x0, waiting for transfers between devices: 50.1 us -> none  [all_blocks(): tiles = lax.all_gather(tiles, axes[k], axis=0, tiled=True)]
    all_to_all x2, waiting for transfers between devices: 29.8 us -> 79.9 us  [from_everyone(): lax.all_to_all(jnp.broadcast_to(array[None], (length, *array.shape)), axi...]
    all_to_all x0 -> x3, starting transfers between devices: none -> 16.1 us  [all_blocks(): lax.all_to_all(jnp.stack([tiles] * lax.axis_size(axes[k])), axes[k], 0, 0)]
    all_to_all x1, starting transfers between devices: 17.6 us -> 8.63 us  [on_device(): lax.all_to_all(qkv, CTX, split_axis=2, concat_axis=1, tiled=True)]
    all_gather x1 -> x0, blocking collectives: 8.3 us -> none  [all_blocks(): tiles = lax.all_gather(tiles, axes[k], axis=0, tiled=True)]
    another operation x0 -> x2, local copies, waits for them, and re-layouts: none -> 6.29 us  [all_blocks(): jnp.stack([tiles] * lax.axis_size(axes[k]))]
  transfers between devices with their start and end apart: 6 -> 7, of which waited for: 4 -> 4; matrix products, arithmetic and copies ran while one was open for 27% -> 23% of each run, Pallas kernels for 0% -> 0%
where the time goes in v1:
time: 400 us; the launch traced here: 395 us
  waiting for transfers between devices  180 us (45%)
  local copies, waits for them, and re-layouts  62.1 us (16%)
  matrix products  53.3 us (13%)
  blocking collectives  46.6 us (12%)
  starting transfers between devices  43 us (11%)
  other arithmetic  7.47 us (2%)
    all_to_all x2, waiting for transfers between devices, from_everyone(): lax.all_to_all(jnp.broadcast_to(array[None], (length, *array.shape)), axi...  79.9 us
    all_to_all x3, waiting for transfers between devices, all_blocks(): lax.all_to_all(jnp.stack([tiles] * lax.axis_size(axes[k])), axes[k], 0, 0)  62.7 us
    all_to_all x1, waiting for transfers between devices, on_device(): lax.all_to_all(qkv, CTX, split_axis=2, concat_axis=1, tiled=True)  37.4 us
    dot_general x27, matrix products, on_device(): jnp.dot(slab, conv_weight[lag, row, col], preferred_element_type=jnp.floa...  35.7 us
    all_to_all x1, blocking collectives, attend(): return lax.all_to_all(out, CTX, split_axis=1, concat_axis=2, tiled=True)  25.2 us
    all_to_all x1, blocking collectives, on_device(): mixed = lax.all_to_all(mixed, 'dp', split_axis=0, concat_axis=3, tiled=True)  21.4 us
    all_to_all x3, starting transfers between devices, all_blocks(): lax.all_to_all(jnp.stack([tiles] * lax.axis_size(axes[k])), axes[k], 0, 0)  16.1 us
    slice x2, local copies, waits for them, and re-layouts, on_device(): padded[2 - lag:2 - lag + f_dev, row:row + height, col:col + width, :]  15.1 us
  transfers between devices with their start and end apart: 7, of which 4 were waited for; matrix products, arithmetic and copies ran while one was open for 23% of the time, Pallas kernels for 0%

profile of v1, /device:TPU:1, one launch (start us, length us, event | category | flops | bytes accessed | tf_op | source)
XLA Modules:
  0.0 394.7 jit_solution(13035748913887990502)
XLA Ops:
  0.7 2.2 fusion.9
  2.9 4.4 %collective-permute-start = (bf16[1,2,16,16,512]{4,3,2,1,0:T(8,128)(2,1)S(1)}, bf16[1,2,16,16,512]{4,3,2,1,0:T(8,128)(2,1)S(1)}, u32[]{:S(2)}, u32[]{:S(2)}) collective-permute-start(bf16[1,2,16,16,512]{4,3,2,1,0:T(8,128)(2,1)S(1)} %slice.235), channel_id=1, source_target_pairs={{0,1},{1,2},{2,3},{3,4},{4,5},{5,6},{6,7},{7,8},{8,9},{9,10},{10,1... | collective-permute-start | bytes 1572872 | tf_op jit(solution)/shard_map/ppermute | solution.py:14
  8.1 4.0 %all-to-all-start.1 = ((bf16[2,1,96,1152]{3,2,1,0:T(8,128)(2,1)}), bf16[2,1,96,1152]{3,2,1,0:T(8,128)(2,1)S(1)}, u32[]{:S(2)}, u32[]{:S(2)}) async-start(bf16[2,1,96,1152]{3,2,1,0:T(8,128)(2,1)} %pad_maximum_fusion.1), calls=%async_computation.1 | async-start | bytes 884736 | tf_op jit(solution)/shard_map/all_to_all | solution.py:39
  12.9 6.6 %all-to-all-done.1 = bf16[2,1,96,1152]{3,2,1,0:T(8,128)(2,1)S(1)} async-done(((bf16[2,1,96,1152]{3,2,1,0:T(8,128)(2,1)}), bf16[2,1,96,1152]{3,2,1,0:T(8,128)(2,1)S(1)}, u32[]{:S(2)}, u32[]{:S(2)}) %all-to-all-start.1) | async-done | bytes 442400 | tf_op jit(solution)/shard_map/all_to_all | solution.py:39
  19.5 1.4 stack.10
  20.9 4.4 %all-to-all-start.2 = ((bf16[4,2,96,1152]{3,2,1,0:T(8,128)(2,1)}), bf16[4,2,96,1152]{3,2,1,0:T(8,128)(2,1)}, u32[]{:S(2)}, u32[]{:S(2)}) async-start(bf16[4,2,96,1152]{3,2,1,0:T(8,128)(2,1)} %stack.10), calls=%async_computation.2 | async-start | bytes 3538944 | tf_op jit(solution)/shard_map/all_to_all | solution.py:39
  25.6 11.3 %pad_slice_fusion = (bf16[5,16,16,512]{3,2,1,0:T(8,128)(2,1)}, bf16[5,16,16,512]{3,2,1,0:T(8,128)(2,1)}, bf16[5,16,16,512]{3,2,1,0:T(8,128)(2,1)}, bf16[5,16,16,...) fusion(bf16[7,16,16,512]{3,2,1,0:T(8,128)(2,1)S(1)} %fusion.15), kind=kLoop, calls=%fused_computation.1 | loop fusion | bytes 26738688 | tf_op jit(solution)/shard_map/slice | solution.py:98
  36.8 3.8 pad_slice_fusion.1
  42.8 0.9 convolution_add_fusion.24
  49.0 0.9 convolution_add_fusion.19
  50.3 0.9 convolution_add_fusion.18
  51.6 2.4 convolution_add_fusion.17
  54.0 0.9 convolution_add_fusion.16
  56.7 0.9 convolution_add_fusion.14
  57.5 1.3 fusion.19
  58.8 0.9 convolution_add_fusion.13
  63.3 2.4 convolution_add_fusion.10
  65.6 0.9 convolution_add_fusion.8
  66.5 4.9 %stack.11 = bf16[4,8,96,1152]{3,2,1,0:T(8,128)(2,1)} broadcast(bf16[8,96,1152]{2,1,0:T(8,128)(2,1)} %bitcast.64), dimensions={1,2,3} | broadcast | bytes 8847360 | tf_op jit(solution)/shard_map/stack | solution.py:39
  71.4 7.7 %all-to-all-start.3 = ((bf16[4,8,96,1152]{3,2,1,0:T(8,128)(2,1)}), bf16[4,8,96,1152]{3,2,1,0:T(8,128)(2,1)}, u32[]{:S(2)}, u32[]{:S(2)}) async-start(bf16[4,8,96,1152]{3,2,1,0:T(8,128)(2,1)} %stack.11), calls=%async_computation.3 | async-start | bytes 14155776 | tf_op jit(solution)/shard_map/all_to_all | solution.py:39
  79.1 2.4 convolution_add_fusion.7
  81.6 2.0 convolution_add_fusion.6
  83.6 2.0 convolution_add_fusion.5
  85.6 2.0 convolution_add_fusion.4
  87.6 2.0 convolution_add_fusion.3
  89.6 2.1 convolution_add_fusion.2
  92.7 2.0 fusion.4
  94.7 2.0 fusion.2
  97.3 1.0 copy-done.21
  100.9 56.0 %all-to-all-done.3 = bf16[4,8,96,1152]{3,2,1,0:T(8,128)(2,1)} async-done(((bf16[4,8,96,1152]{3,2,1,0:T(8,128)(2,1)}), bf16[4,8,96,1152]{3,2,1,0:T(8,128)(2,1)}, u32[]{:S(2)}, u32[]{:S(2)}) %all-to-all-start.3) | async-done | bytes 7077920 | tf_op jit(solution)/shard_map/all_to_all | solution.py:39
  157.0 4.1 %broadcast_in_dim.18 = bf16[4,1,320,3072]{3,2,1,0:T(8,128)(2,1)} broadcast(bf16[320,3072]{1,0:T(8,128)(2,1)S(1)} %multiply_convert_fusion), dimensions={2,3} | broadcast | bytes 9830400 | tf_op jit(solution)/shard_map/broadcast_in_dim | solution.py:20
  161.0 9.6 %all-to-all-start = ((bf16[4,1,320,3072]{3,2,1,0:T(8,128)(2,1)}), bf16[4,1,320,3072]{3,2,1,0:T(8,128)(2,1)}, u32[]{:S(2)}, u32[]{:S(2)}) async-start(bf16[4,1,320,3072]{3,2,1,0:T(8,128)(2,1)} %broadcast_in_dim.18), calls=%async_computation | async-start | bytes 15728640 | tf_op jit(solution)/shard_map/all_to_all | solution.py:19
  170.6 6.7 %copy.61 = bf16[2,4,4,96,1152]{4,3,2,1,0:T(8,128)(2,1)} copy(bf16[2,4,4,96,1152]{4,3,0,1,2:T(8,128)(2,1)} %bitcast.66) | data formatting | bytes 14155776 | tf_op jit(solution)/shard_map/transpose | solution.py:44
  177.4 79.9 %all-to-all-done = bf16[4,1,320,3072]{3,2,1,0:T(8,128)(2,1)} async-done(((bf16[4,1,320,3072]{3,2,1,0:T(8,128)(2,1)}), bf16[4,1,320,3072]{3,2,1,0:T(8,128)(2,1)}, u32[]{:S(2)}, u32[]{:S(2)}) %all-to-all-start) | async-done | bytes 7864352 | tf_op jit(solution)/shard_map/all_to_all | solution.py:19
  257.8 4.3 %all-to-all-start.5 = ((s32[4,1,1]{2,1,0:T(1,128)}), s32[4,1,1]{2,1,0:T(1,128)S(1)}, u32[]{:S(2)}, u32[]{:S(2)}) async-start(s32[4,1,1]{2,1,0:T(1,128)} %broadcast_in_dim.19), calls=%async_computation.5 | async-start | bytes 4096 | tf_op jit(solution)/shard_map/all_to_all | solution.py:19
  262.2 14.7 %convolution_convert_fusion = bf16[1280,1152]{1,0:T(8,128)(2,1)S(1)} fusion(bf16[1280,3072]{1,0:T(8,128)(2,1)} %bitcast.61, bf16[3072,1152]{1,0:T(8,128)(2,1)} %bitcast.180), kind=kOutput, calls=%fused_computation.25 | convolution fusion | flops 9061171200 | bytes 17891328 | tf_op jit(solution)/shard_map/dot_general | solution.py:130
  276.9 4.3 %reshape.226 = bf16[4,5,64,3,384]{4,3,2,1,0:T(4,128)(2,1)} reshape(bf16[1280,1152]{1,0:T(8,128)(2,1)S(1)} %convolution_convert_fusion) | data formatting | bytes 5898240 | tf_op jit(solution)/shard_map/reshape | solution.py:133
  281.2 7.5 %copy.62 = bf16[4,5,64,3,384]{4,0,3,1,2:T(4,128)(2,1)} copy(bf16[4,5,64,3,384]{4,3,2,1,0:T(4,128)(2,1)} %reshape.226) | data formatting | bytes 5898240 | tf_op jit(solution)/shard_map/reshape | solution.py:133
  288.8 8.6 %all-to-all-start.4 = ((bf16[4,5,64,3,384]{4,0,3,1,2:T(4,128)(2,1)}), bf16[4,5,64,3,384]{4,0,3,1,2:T(4,128)(2,1)S(1)}, u32[]{:S(2)}, u32[]{:S(2)}) async-start(bf16[4,5,64,3,384]{4,0,3,1,2:T(4,128)(2,1)} %copy.62), calls=%async_computation.4 | async-start | bytes 5898240 | tf_op jit(solution)/shard_map/all_to_all | solution.py:136
  297.9 37.4 %all-to-all-done.4 = bf16[4,5,64,3,384]{4,0,3,1,2:T(4,128)(2,1)S(1)} async-done(((bf16[4,5,64,3,384]{4,0,3,1,2:T(4,128)(2,1)}), bf16[4,5,64,3,384]{4,0,3,1,2:T(4,128)(2,1)S(1)}, u32[]{:S(2)}, u32[]{:S(2)}) %all-to-all-start.4) | async-done | bytes 2949152 | tf_op jit(solution)/shard_map/all_to_all | solution.py:136
  335.2 2.3 copy.63
  337.5 2.1 fusion.83
  340.3 1.4 fusion.84
  341.7 1.0 fusion.17
  343.5 25.2 %all_to_all.77 = bf16[4,160,2,3,128]{4,0,3,2,1:T(4,128)(2,1)S(1)} all-to-all(bf16[4,160,2,3,128]{4,0,3,2,1:T(4,128)(2,1)S(1)} %copy.68), channel_id=1, replica_groups=mesh['dp'=4,'ctx_0'=2,'ctx_1'=4,'ctx_2'=4] {'ctx_0','ctx_1','ctx_2'}, dimensions={1} | all-to-all | bytes 1966080 | tf_op jit(solution)/shard_map/all_to_all | solution.py:72
  369.5 1.1 copy.70
  370.6 21.4 %all_to_all.78 = bf16[4,5,64,3,128]{4,2,3,1,0:T(8,128)(2,1)S(1)} all-to-all(bf16[4,5,64,3,128]{4,2,3,1,0:T(8,128)(2,1)S(1)} %bitcast.209), channel_id=1, replica_groups=mesh['dp'=4,'ctx_0'=2,'ctx_1'=4,'ctx_2'=4] {'dp'}, dimensions={0} | all-to-all | bytes 1966080 | tf_op jit(solution)/shard_map/all_to_all | solution.py:137
  392.8 1.6 reshape.227
  (108 shorter events, 22.9 us)
Async XLA Ops:
  0.6 98.9 %copy-start = (bf16[64,3072]{1,0:T(8,128)(2,1)S(1)}, bf16[64,3072]{1,0:T(8,128)(2,1)}, u32[]{:S(2)}) copy-start(bf16[64,3072]{1,0:T(8,128)(2,1)} %param.13) | copy-start | bytes 1179652
  0.6 6.6 %copy-start.28 = (bf16[96,1152]{1,0:T(8,128)(2,1)S(1)}, bf16[96,1152]{1,0:T(8,128)(2,1)}, u32[]{:S(2)}) copy-start(bf16[96,1152]{1,0:T(8,128)(2,1)} %param.15) | copy-start | bytes 663556
  2.9 22.5 %collective-permute-start = (bf16[1,2,16,16,512]{4,3,2,1,0:T(8,128)(2,1)S(1)}, bf16[1,2,16,16,512]{4,3,2,1,0:T(8,128)(2,1)S(1)}, u32[]{:S(2)}, u32[]{:S(2)}) collective-permute-start(bf16[1,2,16,16,512]{4,3,2,1,0:T(8,128)(2,1)S(1)} %slice.235), channel_id=1, source_target_pairs={{0,1},{1,2},{2,3},{3,4},{4,5},{5,6},{6,7},{7,8},{8,9},{9,10},{10,1... | collective-permute-start | bytes 1572872 | tf_op jit(solution)/shard_map/ppermute | solution.py:14
  8.1 11.4 %all-to-all-start.1 = ((bf16[2,1,96,1152]{3,2,1,0:T(8,128)(2,1)}), bf16[2,1,96,1152]{3,2,1,0:T(8,128)(2,1)S(1)}, u32[]{:S(2)}, u32[]{:S(2)}) async-start(bf16[2,1,96,1152]{3,2,1,0:T(8,128)(2,1)} %pad_maximum_fusion.1), calls=%async_computation.1 | async-start | bytes 884736 | tf_op jit(solution)/shard_map/all_to_all | solution.py:39
  20.9 45.6 %all-to-all-start.2 = ((bf16[4,2,96,1152]{3,2,1,0:T(8,128)(2,1)}), bf16[4,2,96,1152]{3,2,1,0:T(8,128)(2,1)}, u32[]{:S(2)}, u32[]{:S(2)}) async-start(bf16[4,2,96,1152]{3,2,1,0:T(8,128)(2,1)} %stack.10), calls=%async_computation.2 | async-start | bytes 3538944 | tf_op jit(solution)/shard_map/all_to_all | solution.py:39
  25.3 15.3 %slice-start = ((s8[14155776]{0:T(1024)(128)(4,1)}), s8[4194304]{0:T(1024)(128)(4,1)S(1)}, s32[]{:S(2)}) async-start(s8[14155776]{0:T(1024)(128)(4,1)} %bitcast.175), calls=%async_computation.8 | async-start | bytes 8388608
  25.5 15.1 %slice-start.1 = ((s8[14155776]{0:T(1024)(128)(4,1)}), s8[4194304]{0:T(1024)(128)(4,1)S(1)}, s32[]{:S(2)}) async-start(s8[14155776]{0:T(1024)(128)(4,1)} %bitcast.175), calls=%async_computation.9 | async-start | bytes 8388608
  25.5 15.1 %slice-start.2 = ((s8[14155776]{0:T(1024)(128)(4,1)}), s8[4194304]{0:T(1024)(128)(4,1)S(1)}, s32[]{:S(2)}) async-start(s8[14155776]{0:T(1024)(128)(4,1)} %bitcast.175), calls=%async_computation.10 | async-start | bytes 8388608
  25.5 15.1 %slice-start.3 = ((s8[14155776]{0:T(1024)(128)(4,1)}), s8[1572864]{0:T(1024)(128)(4,1)S(1)}, s32[]{:S(2)}) async-start(s8[14155776]{0:T(1024)(128)(4,1)} %bitcast.175), calls=%async_computation.11 | async-start | bytes 3145728
  41.5 1.3 copy-start.16
  42.8 1.3 copy-start.15
  44.1 1.3 copy-start.14
  46.3 1.3 copy-start.13
  47.6 1.3 copy-start.12
  49.0 1.3 copy-start.11
  50.3 1.3 copy-start.10
  51.6 2.4 copy-start.9
  54.0 1.3 copy-start.8
  55.3 1.3 copy-start.7
  58.8 1.3 copy-start.6
  60.1 1.3 copy-start.17
  61.0 1.4 copy-start.5
  63.3 2.4 copy-start.4
  71.4 85.5 %all-to-all-start.3 = ((bf16[4,8,96,1152]{3,2,1,0:T(8,128)(2,1)}), bf16[4,8,96,1152]{3,2,1,0:T(8,128)(2,1)}, u32[]{:S(2)}, u32[]{:S(2)}) async-start(bf16[4,8,96,1152]{3,2,1,0:T(8,128)(2,1)} %stack.11), calls=%async_computation.3 | async-start | bytes 14155776 | tf_op jit(solution)/shard_map/all_to_all | solution.py:39
  79.1 2.4 copy-start.26
  81.6 2.0 copy-start.22
  83.6 2.0 copy-start.25
  85.6 2.0 copy-start.24
  87.6 2.0 copy-start.23
  89.6 2.1 copy-start.2
  89.6 2.7 copy-start.3
  89.6 3.0 copy-start.19
  92.7 2.0 copy-start.18
  94.7 2.0 copy-start.20
  96.7 1.7 copy-start.29
  97.3 1.1 copy-start.21
  97.3 2.2 copy-start.27
  99.5 0.8 copy-start.30
  161.0 96.2 %all-to-all-start = ((bf16[4,1,320,3072]{3,2,1,0:T(8,128)(2,1)}), bf16[4,1,320,3072]{3,2,1,0:T(8,128)(2,1)}, u32[]{:S(2)}, u32[]{:S(2)}) async-start(bf16[4,1,320,3072]{3,2,1,0:T(8,128)(2,1)} %broadcast_in_dim.18), calls=%async_computation | async-start | bytes 15728640 | tf_op jit(solution)/shard_map/all_to_all | solution.py:19
  257.8 30.9 %all-to-all-start.5 = ((s32[4,1,1]{2,1,0:T(1,128)}), s32[4,1,1]{2,1,0:T(1,128)S(1)}, u32[]{:S(2)}, u32[]{:S(2)}) async-start(s32[4,1,1]{2,1,0:T(1,128)} %broadcast_in_dim.19), calls=%async_computation.5 | async-start | bytes 4096 | tf_op jit(solution)/shard_map/all_to_all | solution.py:19
  288.8 46.4 %all-to-all-start.4 = ((bf16[4,5,64,3,384]{4,0,3,1,2:T(4,128)(2,1)}), bf16[4,5,64,3,384]{4,0,3,1,2:T(4,128)(2,1)S(1)}, u32[]{:S(2)}, u32[]{:S(2)}) async-start(bf16[4,5,64,3,384]{4,0,3,1,2:T(4,128)(2,1)} %copy.62), calls=%async_computation.4 | async-start | bytes 5898240 | tf_op jit(solution)/shard_map/all_to_all | solution.py:136
  370.6 23.9 %copy-start.1 = (bf16[64,3072]{1,0:T(8,128)(2,1)S(1)}, bf16[64,3072]{1,0:T(8,128)(2,1)}, u32[]{:S(2)}) copy-start(bf16[64,3072]{1,0:T(8,128)(2,1)} %param.13) | copy-start | bytes 1179652
